TPU v7x, 32 devices: a whole 2x2x4 slice. The times are simulated.
32 devices in a mesh: grp: 4 (over y, x), dev: 8 (over z, core).
Axes of the slice: x: 2, y: 2, z: 4, core: 2. Of those that a mesh axis runs over, the one named last changes fastest.
Arguments:
- queries: bfloat16 [4096, 256], P(('grp', 'dev')), may hold values from -32 to 32
- items: bfloat16 [4096, 256], P(('grp', 'dev')), may hold values from -24 to 24
- item_ids: int32 [4096], P('grp'), may hold values from 0 to 262143
- neg_embed: bfloat16 [4096, 256], P('dev'), may hold values from -6 to 6
- neg_logq: float32 [4096], P('dev'), may hold values from -12 to -8
- logq_table: float32 [262144], replicated, may hold values from -11 to -9.5
Outputs:
- query_loss: float32 [4096], P(('grp', 'dev'))
- query_grad: float32 [4096, 256], P(('grp', 'dev'))
- item_grad: float32 [4096, 256], P(('grp', 'dev'))
- negative_grad: float32 [4096, 256], P('dev')
Inputs may be any that keep to these rules, and one draw needn't show every extreme that they name: `item_ids`: a row of logq_table.
All inputs are finite; a program needn't handle non-finite values.
Results may differ from a plain program's by a relative error of at most 0.0036.
Values may be sent and summed in bfloat16 or wider, within the bound.
No kernel may reach another device: no remote copies, remote signals or barrier semaphores. Data moves between devices by JAX's collectives and lax.ppermute only.
A program may use at most 64 MiB of HBM per device.

v0:
```python
import jax
import jax.numpy as jnp
from jax import lax
from jax.sharding import PartitionSpec as P

logit_scale = 0.25


def block_shape(all_rows):
    block_rows = min(512, all_rows)
    return (block_rows, all_rows // block_rows)


def log_total(maxima, totals):
    row_max = lax.pmax(maxima, "dev")
    row_sum = lax.psum(totals * jnp.exp(maxima - row_max), "dev")
    return row_max + jnp.log(row_sum)


def row_stats(scores):
    row_max = jnp.max(scores, axis=1)
    return (row_max, jnp.sum(jnp.exp(scores - row_max[:, None]), axis=1))


def logits(q_block, candidates, cand_offsets):
    return (
        logit_scale * jnp.dot(q_block, candidates.T, preferred_element_type=jnp.float32)
        - cand_offsets[None, :]
    )


def local(queries, items, item_ids, neg_embed, neg_logq, logq_table):
    own_rows, feat_width = queries.shape
    dev_index = lax.axis_index("dev")
    own_start = dev_index * own_rows
    own_ids = lax.dynamic_slice_in_dim(item_ids, own_start, own_rows, 0)
    own_offsets = jnp.take(logq_table, own_ids, axis=0)
    group_q = lax.all_gather(queries, "dev", axis=0, tiled=True)
    all_rows = group_q.shape[0]
    block_rows, block_count = block_shape(all_rows)
    blocks = group_q.reshape(block_count, block_rows, feat_width)
    starts = jnp.arange(block_count, dtype=jnp.int32) * block_rows
    candidates = jnp.concatenate([items, neg_embed], axis=0)
    cand_offsets = jnp.concatenate([own_offsets, neg_logq], axis=0)
    columns = jnp.arange(candidates.shape[0], dtype=jnp.int32)

    def positives(first_row):
        targets = first_row + jnp.arange(block_rows, dtype=jnp.int32) - own_start
        return (columns[None, :] == targets[:, None]) & (columns[None, :] < own_rows)

    def forward(packed):
        q_block, first_row = packed
        scores = logits(q_block, candidates, cand_offsets)
        row_max, row_sum = row_stats(scores)
        return (row_max, row_sum, jnp.sum(jnp.where(positives(first_row), scores, 0.0), axis=1))

    maxima, totals, matched = lax.map(forward, (blocks, starts))
    log_norm = log_total(maxima.reshape(all_rows), totals.reshape(all_rows))
    own_norm = lax.dynamic_slice_in_dim(log_norm, own_start, own_rows, 0)
    own_match = lax.dynamic_slice_in_dim(matched.reshape(all_rows), own_start, own_rows, 0)
    query_loss = own_norm - own_match

    def backward(summed, packed):
        q_block, first_row, block_norm = packed
        scores = logits(q_block, candidates, cand_offsets)
        logit_grad = (
            logit_scale
            * (jnp.exp(scores - block_norm[:, None]) - positives(first_row).astype(jnp.float32))
        ).astype(jnp.bfloat16)
        summed = summed + jnp.einsum(
            "rc,rd->cd", logit_grad, q_block, preferred_element_type=jnp.float32
        )
        return (summed, jnp.dot(logit_grad, candidates, preferred_element_type=jnp.float32))

    zero_acc = jnp.zeros((candidates.shape[0], feat_width), jnp.float32)
    cand_grad, q_partial = lax.scan(
        backward, zero_acc, (blocks, starts, log_norm.reshape(block_count, block_rows))
    )
    query_grad = lax.psum_scatter(
        q_partial.reshape(all_rows, feat_width), "dev", scatter_dimension=0, tiled=True
    )
    item_grad = cand_grad[:own_rows]
    negative_part = cand_grad[own_rows:]
    negative_grad = lax.psum(negative_part, "grp")
    return (query_loss, query_grad, item_grad, negative_grad)


def solution(mesh):
    return jax.shard_map(
        local,
        mesh=mesh,
        in_specs=(
            P(("grp", "dev"), None),
            P(("grp", "dev"), None),
            P("grp"),
            P("dev", None),
            P("dev"),
            P(),
        ),
        out_specs=(
            P(("grp", "dev")),
            P(("grp", "dev"), None),
            P(("grp", "dev"), None),
            P("dev", None),
        ),
        check_vma=False,
    )
```

profile of v0, /device:TPU:0, one launch (start us, length us, event | category | flops | bytes accessed | tf_op | source)
XLA Modules:
  0.0 128.1 jit_solution(7890898230688318742)
XLA Ops:
  8.0 0.0 copy-start
  8.0 0.0 copy-start.3
  8.0 0.0 all-reduce.2.cloned.1.call-start
  8.1 0.8 compare_select_fusion
  9.0 0.3 copy-done
  9.2 1.1 gather_fusion
  10.4 0.8 and_select_fusion
  11.2 0.8 constant_dynamic-update-slice_fusion.1
  12.0 16.7 %all_gather.3 = bf16[1024,256]{1,0:T(8,128)(2,1)S(1)} all-gather(bf16[128,256]{1,0:T(8,128)(2,1)} %param.10), channel_id=1, replica_groups=mesh['grp'=4,'dev'=8] {'dev'}, dimensions={0}, use_global_device_ids=true | all-gather | bytes 589824 | tf_op jit(solution)/shard_map/all_gather | solution.py:38
  28.7 0.7 pad_maximum_fusion
  29.4 0.0 copy-done.3
  29.4 5.2 %while.30 = (s32[]{:T(128)}, f32[2,512]{1,0:T(2,128)S(1)}, f32[2,512]{1,0:T(2,128)S(1)}, f32[2,512]{1,0:T(2,128)S(1)}, bf16[2,512,256]{2,1,0:T(8,128)(2,1)S(1)},...) while((s32[]{:T(128)}, f32[2,512]{1,0:T(2,128)S(1)}, ...), condition=%wide.region_4.5_spmd.clone.clone, body=%wide.region_0.4_spmd.clone.clone.sunk | while | flops 170721408 | bytes 3241369 | solution.py:57
  29.4 0.6 dynamic_slice.67
  30.0 0.6 add_subtract_fusion.4
  30.7 0.5 fusion.40
  31.2 0.7 select_reduce_fusion.2
  32.0 0.6 dynamic_slice.67
  32.6 0.6 add_subtract_fusion.4
  33.3 0.5 fusion.40
  33.8 0.7 select_reduce_fusion.2
  34.6 17.0 %pmax.7 = f32[1024]{0:T(1024)S(1)} all-reduce(f32[1024]{0:T(1024)S(1)} %bitcast.69), channel_id=1, replica_groups=mesh['grp'=4,'dev'=8] {'dev'}, use_global_device_ids=true, to_apply=%region_5.6 | all-reduce | flops 1024 | bytes 8192 | tf_op jit(solution)/shard_map/pmax | solution.py:15
  51.6 13.6 %psum.14 = f32[1024]{0:T(1024)S(1)} all-reduce(f32[1024]{0:T(1024)S(1)} %exponential_multiply_fusion), channel_id=1, replica_groups=mesh['grp'=4,'dev'=8] {'dev'}, use_global_device_ids=true, to_apply=%region_6.7 | all-reduce | flops 1024 | bytes 8192 | tf_op jit(solution)/shard_map/psum | solution.py:16
  65.2 9.0 %while.31 = (s32[]{:T(128)}, f32[640,256]{1,0:T(8,128)S(1)}, f32[2,512,256]{2,1,0:T(8,128)}, bf16[2,512,256]{2,1,0:T(8,128)(2,1)S(1)}, bf16[640,256]{1,0:T(8,128...) while((s32[]{:T(128)}, f32[640,256]{1,0:T(8,128)S(1)}, ...), condition=%wide.region_8.9_spmd.clone.clone, body=%wide.region_7.8_spmd.clone.clone.sunk | while | flops 506594944 | bytes 13385563 | solution.py:76
  65.2 0.6 dynamic_slice.71
  65.8 0.6 add_subtract_fusion.5
  66.5 0.6 fusion.47
  67.1 0.0 copy-start.1
  67.1 0.5 convolution_add_fusion.2
  67.7 0.7 copy-done.1
  68.4 0.4 fusion.48
  68.7 0.0 copy-start.2
  68.7 1.0 copy-done.2
  69.7 0.6 dynamic_slice.71
  70.3 0.6 add_subtract_fusion.5
  71.0 0.6 fusion.47
  71.6 0.0 copy-start.1
  71.6 0.5 convolution_add_fusion.2
  72.2 0.7 copy-done.1
  72.9 0.4 fusion.48
  73.2 1.0 copy-done.2
  74.2 0.8 slice.7
  75.0 0.0 all-reduce.2.cloned.1.call-update
  75.1 0.0 reduce-scatter.2.cloned.1.call-start
  75.1 0.5 reduce-scatter.2.cloned.1.call-update
  75.7 0.7 slice.6
  76.3 0.6 dynamic-slice_subtract_fusion
  76.9 41.9 %all-reduce.2.cloned.1.call-done = f32[512,256]{1,0:T(8,128)} async-done(((f32[512,256]{1,0:T(8,128)}), f32[512,256]{1,0:T(8,128)}) %all-reduce.2.cloned.1.call-update) | async-done | bytes 524304 | tf_op jit(solution)/shard_map/psum | solution.py:84
  118.8 1.9 %copy.40 = f32[512,256]{1,0:T(8,128)} copy(f32[512,256]{1,0:T(8,128)} %all-reduce.2.cloned.1.call-done) | data formatting | bytes 1048576
  (28 shorter events, 0.4 us)
Async XLA Ops:
  8.0 1.2 copy-start
  8.0 21.4 %copy-start.3 = (bf16[512,256]{1,0:T(8,128)(2,1)S(1)}, bf16[512,256]{1,0:T(8,128)(2,1)}, u32[]{:S(2)}) copy-start(bf16[512,256]{1,0:T(8,128)(2,1)} %param.13) | copy-start | bytes 786436
  8.0 110.8 %all-reduce.2.cloned.1.call-start = ((), (), s32[]{:S(2)}) async-start(), calls=%async_computation.2 | async-start | bytes 1048576 | tf_op jit(solution)/shard_map/psum | solution.py:84
  67.1 1.2 copy-start.1
  68.7 1.0 copy-start.2
  71.6 1.2 copy-start.1
  73.2 1.0 copy-start.2
  75.1 43.7 %reduce-scatter.2.cloned.1.call-start = ((), (), s32[]{:S(2)}) async-start(), calls=%async_computation.1 | async-start | bytes 1179648 | tf_op jit(solution)/shard_map/reduce_scatter | solution.py:79
Sparse Core Ops, SparseCore 0:
  75.2 43.5 all-reduce.1
Sparse Core Ops, SparseCore 1:
  78.4 30.7 reduce-scatter.1
where the time goes:
time: 129 us; the launch traced here: 128 us
  blocking collectives  47.3 us (37%)
  waiting for transfers between devices  42.4 us (33%)
  between operations  15.6 us (12%)
  local copies, waits for them, and re-layouts  11.6 us (9%)
  other arithmetic  6.94 us (5%)
  matrix products  4.02 us (3%)
    psum x1, waiting for transfers between devices, local(): negative_grad = lax.psum(negative_part, 'grp')  41.9 us
    pmax x1, blocking collectives, log_total(): row_max = lax.pmax(maxima, 'dev')  17 us
    all_gather x1, blocking collectives, local(): group_q = lax.all_gather(queries, 'dev', axis=0, tiled=True)  16.7 us
    psum x1, blocking collectives, log_total(): row_sum = lax.psum(totals * jnp.exp(maxima - row_max), 'dev')  13.6 us
    while x8, local copies, waits for them, and re-layouts  3.35 us
    unnamed x9, local copies, waits for them, and re-layouts  2.99 us
    sub x4, other arithmetic, positives(): targets = first_row + jnp.arange(block_rows, dtype=jnp.int32) - own_start  2.59 us
  transfers between devices with their start and end apart: 2, of which 1 were waited for; matrix products, arithmetic and copies ran while one was open for 1% of the time, Pallas kernels for 0%

commit v1 on v0

--- a/solution.py
+++ b/solution.py
@@ -81,7 +81,7 @@
     )
     item_grad = cand_grad[:own_rows]
     negative_part = cand_grad[own_rows:]
-    negative_grad = lax.psum(negative_part, "grp")
+    negative_grad = jnp.sum(lax.all_gather(negative_part, "grp"), axis=0)
     return (query_loss, query_grad, item_grad, negative_grad)
 
 

time: 129 us -> 119 us (0.922)
  waiting for transfers between devices: 42.4 us -> 32.2 us
  other arithmetic: 6.94 us -> 9.54 us
  local copies, waits for them, and re-layouts: 11.6 us -> 9.74 us
    psum x1 -> x0, waiting for transfers between devices: 41.9 us -> none  [local(): negative_grad = lax.psum(negative_part, 'grp')]
    all_gather x0 -> x1, waiting for transfers between devices: none -> 31.7 us  [local(): negative_grad = jnp.sum(lax.all_gather(negative_part, 'grp'), axis=0)]
    reduce_sum x0 -> x1, other arithmetic: none -> 2.6 us  [local(): negative_grad = jnp.sum(lax.all_gather(negative_part, 'grp'), axis=0)]
    unnamed x9 -> x8, local copies, waits for them, and re-layouts: 2.99 us -> 1.12 us
  transfers between devices with their start and end apart: 2 -> 2, of which waited for: 1 -> 1; matrix products, arithmetic and copies ran while one was open for 1% -> 3% of each run, Pallas kernels for 0% -> 0%
where the time goes in v1:
time: 119 us
  blocking collectives  47.3 us (40%)
  waiting for transfers between devices  32.2 us (27%)
  between operations  15.6 us (13%)
  local copies, waits for them, and re-layouts  9.74 us (8%)
  other arithmetic  9.54 us (8%)
  matrix products  4.02 us (3%)
    all_gather x1, waiting for transfers between devices, local(): negative_grad = jnp.sum(lax.all_gather(negative_part, 'grp'), axis=0)  31.7 us
    pmax x1, blocking collectives, log_total(): row_max = lax.pmax(maxima, 'dev')  17 us
    all_gather x1, blocking collectives, local(): group_q = lax.all_gather(queries, 'dev', axis=0, tiled=True)  16.7 us
    psum x1, blocking collectives, log_total(): row_sum = lax.psum(totals * jnp.exp(maxima - row_max), 'dev')  13.6 us
    while x8, local copies, waits for them, and re-layouts  3.34 us
    reduce_sum x1, other arithmetic, local(): negative_grad = jnp.sum(lax.all_gather(negative_part, 'grp'), axis=0)  2.6 us
    sub x4, other arithmetic, positives(): targets = first_row + jnp.arange(block_rows, dtype=jnp.int32) - own_start  2.59 us
  transfers between devices with their start and end apart: 2, of which 1 were waited for; matrix products, arithmetic and copies ran while one was open for 3% of the time, Pallas kernels for 0%

profile of v1, /device:TPU:0, one launch (start us, length us, event | category | flops | bytes accessed | tf_op | source)
XLA Modules:
  0.0 118.6 jit_solution(369046078729853366)
XLA Ops:
  8.0 0.0 copy-start
  8.0 0.0 copy-start.3
  8.0 0.0 all-gather.3.cloned.1.call-start
  8.1 0.8 compare_select_fusion
  9.0 0.3 copy-done
  9.2 1.1 gather_fusion
  10.4 0.8 and_select_fusion
  11.2 0.8 constant_dynamic-update-slice_fusion.1
  12.0 16.7 %all_gather.9 = bf16[1024,256]{1,0:T(8,128)(2,1)S(1)} all-gather(bf16[128,256]{1,0:T(8,128)(2,1)} %param.10), channel_id=1, replica_groups=mesh['grp'=4,'dev'=8] {'dev'}, dimensions={0}, use_global_device_ids=true | all-gather | bytes 589824 | tf_op jit(solution)/shard_map/all_gather | solution.py:38
  28.7 0.7 pad_maximum_fusion
  29.4 0.0 copy-done.3
  29.4 5.2 %while.30 = (s32[]{:T(128)}, f32[2,512]{1,0:T(2,128)S(1)}, f32[2,512]{1,0:T(2,128)S(1)}, f32[2,512]{1,0:T(2,128)S(1)}, bf16[2,512,256]{2,1,0:T(8,128)(2,1)S(1)},...) while((s32[]{:T(128)}, f32[2,512]{1,0:T(2,128)S(1)}, ...), condition=%wide.region_4.5_spmd.clone.clone, body=%wide.region_0.4_spmd.clone.clone.sunk | while | flops 170721408 | bytes 3241369 | solution.py:57
  29.4 0.6 dynamic_slice.67
  30.0 0.6 add_subtract_fusion.4
  30.7 0.5 fusion.40
  31.2 0.7 select_reduce_fusion.2
  32.0 0.6 dynamic_slice.67
  32.6 0.6 add_subtract_fusion.4
  33.3 0.5 fusion.40
  33.8 0.7 select_reduce_fusion.2
  34.6 17.0 %pmax.7 = f32[1024]{0:T(1024)S(1)} all-reduce(f32[1024]{0:T(1024)S(1)} %bitcast.71), channel_id=1, replica_groups=mesh['grp'=4,'dev'=8] {'dev'}, use_global_device_ids=true, to_apply=%region_5.6 | all-reduce | flops 1024 | bytes 8192 | tf_op jit(solution)/shard_map/pmax | solution.py:15
  51.6 13.6 %psum.7 = f32[1024]{0:T(1024)S(1)} all-reduce(f32[1024]{0:T(1024)S(1)} %exponential_multiply_fusion), channel_id=1, replica_groups=mesh['grp'=4,'dev'=8] {'dev'}, use_global_device_ids=true, to_apply=%region_6.7 | all-reduce | flops 1024 | bytes 8192 | tf_op jit(solution)/shard_map/psum | solution.py:16
  65.2 9.0 %while.31 = (s32[]{:T(128)}, f32[640,256]{1,0:T(8,128)S(1)}, f32[2,512,256]{2,1,0:T(8,128)}, bf16[2,512,256]{2,1,0:T(8,128)(2,1)S(1)}, bf16[640,256]{1,0:T(8,128...) while((s32[]{:T(128)}, f32[640,256]{1,0:T(8,128)S(1)}, ...), condition=%wide.region_8.9_spmd.clone.clone, body=%wide.region_7.8_spmd.clone.clone.sunk | while | flops 506594944 | bytes 13385563 | solution.py:76
  65.2 0.6 dynamic_slice.71
  65.8 0.6 add_subtract_fusion.5
  66.5 0.6 fusion.47
  67.1 0.0 copy-start.1
  67.1 0.5 convolution_add_fusion.2
  67.7 0.7 copy-done.1
  68.4 0.4 fusion.48
  68.7 0.0 copy-start.2
  68.7 1.0 copy-done.2
  69.7 0.6 dynamic_slice.71
  70.3 0.6 add_subtract_fusion.5
  71.0 0.6 fusion.47
  71.6 0.0 copy-start.1
  71.6 0.5 convolution_add_fusion.2
  72.2 0.7 copy-done.1
  72.8 0.4 fusion.48
  73.2 1.0 copy-done.2
  74.2 0.8 slice.7
  75.0 0.0 all-gather.3.cloned.1.call-update
  75.1 0.0 reduce-scatter.2.cloned.1.call-start
  75.1 0.5 reduce-scatter.2.cloned.1.call-update
  75.6 0.7 slice.6
  76.3 0.6 dynamic-slice_subtract_fusion
  76.9 31.7 %all-gather.3.cloned.1.call-done = f32[2048,256]{1,0:T(8,128)} async-done(((f32[512,256]{1,0:T(8,128)}), f32[2048,256]{1,0:T(8,128)}) %all-gather.3.cloned.1.call-update) | async-done | bytes 2097168 | tf_op jit(solution)/shard_map/all_gather | solution.py:84
  108.6 2.6 %reduce_sum.27 = f32[512,256]{1,0:T(8,128)} reduce(f32[4,512,256]{2,1,0:T(8,128)} %bitcast.65, f32[]{:T(128)} %constant.41.clone.1), dimensions={0}, to_apply=%region_10.11 | reduce | flops 393216 | bytes 2621444 | tf_op jit(solution)/shard_map/reduce_sum | solution.py:84
  (28 shorter events, 0.4 us)
Async XLA Ops:
  8.0 1.2 %copy-start = (f32[262144]{0:T(1024)S(1)}, f32[262144]{0:T(1024)}, u32[]{:S(2)}) copy-start(f32[262144]{0:T(1024)} %param.15) | copy-start | bytes 3145732
  8.0 21.4 %copy-start.3 = (bf16[512,256]{1,0:T(8,128)(2,1)S(1)}, bf16[512,256]{1,0:T(8,128)(2,1)}, u32[]{:S(2)}) copy-start(bf16[512,256]{1,0:T(8,128)(2,1)} %param.13) | copy-start | bytes 786436
  8.0 100.6 %all-gather.3.cloned.1.call-start = ((), (), s32[]{:S(2)}) async-start(), calls=%async_computation.2 | async-start | bytes 2621440 | tf_op jit(solution)/shard_map/all_gather | solution.py:84
  67.1 1.2 %copy-start.1 = (f32[2,512,256]{2,1,0:T(8,128)S(1)}, f32[2,512,256]{2,1,0:T(8,128)}, u32[]{:S(2)}) copy-start(f32[2,512,256]{2,1,0:T(8,128)} %get-tuple-element.426) | copy-start | bytes 3145732 | tf_op jit(solution)/shard_map/while
  68.7 1.0 copy-start.2
  71.6 1.2 %copy-start.1 = (f32[2,512,256]{2,1,0:T(8,128)S(1)}, f32[2,512,256]{2,1,0:T(8,128)}, u32[]{:S(2)}) copy-start(f32[2,512,256]{2,1,0:T(8,128)} %get-tuple-element.426) | copy-start | bytes 3145732 | tf_op jit(solution)/shard_map/while
  73.2 1.0 copy-start.2
  75.1 36.1 %reduce-scatter.2.cloned.1.call-start = ((), (), s32[]{:S(2)}) async-start(), calls=%async_computation.1 | async-start | bytes 1179648 | tf_op jit(solution)/shard_map/reduce_scatter | solution.py:79
Sparse Core Ops, SparseCore 0:
  75.2 33.3 all-gather.2
Sparse Core Ops, SparseCore 1:
  78.4 30.8 reduce-scatter.1
